TPU v7x, 256 devices: a whole 4x4x8 slice. The times are simulated.
256 devices in a mesh: tm: 8 (over z), seq: 32 (over y, x, core).
Axes of the slice: x: 4, y: 4, z: 8, core: 2. Of those that a mesh axis runs over, the one named last changes fastest.
Arguments:
- states: float32 [64, 1536, 64], P('tm', 'seq'), may hold values from -11 to 11
- first_state: float32 [1536, 64], P('seq'), may hold values from -6 to 6
- now_step: int32 [64], P('tm'), may hold values from 1 to 960, as said below
- next_step: int32 [64], P('tm'), may hold values from 0 to 959, as said below
- embed_weight: bfloat16 [64, 1536], replicated, may hold values from -0.75 to 0.75
- mod_weight: bfloat16 [256, 4608], replicated, may hold values from -0.375 to 0.375
- qkv_weight: bfloat16 [1536, 12, 384], P('seq'), may hold values from -1 to 1
- out_weight: bfloat16 [1536, 1536], P('seq'), may hold values from -0.15625 to 0.15625
- final_weight: bfloat16 [1536, 64], replicated, may hold values from -0.15625 to 0.15625
Outputs:
- advanced: float32 [64, 1536, 64], P('tm', 'seq')
- errors: float32 [64], P('tm')
Inputs may be any that keep to these rules, and one draw needn't show every extreme that they name: now_step[0] = 960 and now_step[j + 1] = next_step[j]. next_step[j] is now_step[j] minus a gap of 1 to 15.
All inputs are finite; a program needn't handle non-finite values.
Results may differ from a plain program's by a relative error of at most 0.002.
Values may be sent and summed in bfloat16 or wider, within the bound.
A program may use at most 64 MiB of HBM per device.

v0:
```python
import math
import jax
import jax.numpy as jnp
from jax import lax
from jax.sharding import PartitionSpec as P


def from_behind(shard, axis, by):
    count = lax.axis_size(axis)
    pairs = [(i, i + by) for i in range(count) if 0 <= i + by < count]
    return lax.ppermute(shard, axis, pairs)


def entering(part, axis, combine, identity):
    place = lax.axis_index(axis)
    gathered = lax.all_gather(part, axis)
    state = jnp.zeros_like(part) + jnp.asarray(identity, part.dtype)

    def one(step, state):
        return combine(state, lax.dynamic_index_in_dim(gathered, step, 0, False))

    return lax.fori_loop(0, place, one, state)


def layer_norm(rows):
    row_mean = jnp.mean(rows, axis=-1, keepdims=True)
    centered = rows - row_mean
    variance = jnp.mean(centered * centered, axis=-1, keepdims=True)
    return centered * lax.rsqrt(variance + 1e-06)


def alpha_bar(step_ids):
    fraction = (step_ids.astype(jnp.float32) / 1000.0 + 0.008) / 1.008
    return jnp.cos(fraction * (math.pi / 2)) ** 2


def coefficients(now_step, next_step):
    alpha_now = alpha_bar(now_step)
    alpha_next = alpha_bar(next_step)
    step_ratio = jnp.sqrt(alpha_next / alpha_now)
    keep_coef = step_ratio - 1.0
    noise_coef = jnp.sqrt(1.0 - alpha_next) - step_ratio * jnp.sqrt(1.0 - alpha_now)
    return (keep_coef, noise_coef)


def modulation(step_ids, mod_weight):
    half_freq = mod_weight.shape[0] // 2
    frequency = jnp.exp(-math.log(10000.0) * jnp.arange(half_freq, dtype=jnp.float32) / half_freq)
    angles = step_ids.astype(jnp.float32)[:, None] * frequency[None, :]
    time_embed = jnp.concatenate([jnp.cos(angles), jnp.sin(angles)], axis=1).astype(jnp.bfloat16)
    return jnp.dot(time_embed, mod_weight, preferred_element_type=jnp.float32)


def attend_one(pair_item):
    hdim = pair_item.shape[1] // 3
    length = pair_item.shape[0]
    query_rows = 512
    queries = pair_item[:, :hdim]
    key_rows = pair_item[:, hdim : 2 * hdim]
    values = pair_item[:, 2 * hdim :]

    def one_block(query_block):
        scores = jnp.dot(query_block, key_rows.T, preferred_element_type=jnp.float32) * hdim ** (
            -0.5
        )
        row_max = jnp.max(scores, axis=1, keepdims=True)
        exponent = jnp.exp(scores - row_max)
        weights = (exponent / jnp.sum(exponent, axis=1, keepdims=True)).astype(jnp.bfloat16)
        return jnp.dot(weights, values, preferred_element_type=jnp.float32).astype(jnp.bfloat16)

    blocks_out = lax.map(one_block, queries.reshape(length // query_rows, query_rows, hdim))
    return blocks_out.reshape(length, hdim)


def attend_pairs(pair_block):
    return lax.map(attend_one, pair_block[0])[None]


def add_terms(earlier, later):
    return earlier + later


def per_device(
    states,
    first_state,
    now_step,
    next_step,
    embed_weight,
    mod_weight,
    qkv_weight,
    out_weight,
    final_weight,
):
    step_count, tokd, chans = states.shape
    seq_devs = lax.axis_size("seq")
    time_index = lax.axis_index("tm")
    heads = qkv_weight.shape[1]
    width_three = qkv_weight.shape[2]
    hdim = width_three // 3
    width = heads * hdim
    edge_state = from_behind(states[-1], "tm", 1)
    opening = jnp.where(time_index == 0, first_state, edge_state)
    previous = jnp.concatenate([opening[None], states[:-1]], axis=0)
    keep_coef, noise_coef = coefficients(now_step, next_step)
    modulated_all = modulation(now_step, mod_weight)
    shift_mod = modulated_all[:, :width]
    scale_mod = modulated_all[:, width : 2 * width]
    gate_mod = modulated_all[:, 2 * width :]
    residual = jnp.einsum(
        "tsc,cd->tsd",
        previous.astype(jnp.bfloat16),
        embed_weight,
        preferred_element_type=jnp.float32,
    )
    modulated = (
        layer_norm(residual) * (1.0 + scale_mod[:, None, :]) + shift_mod[:, None, :]
    ).astype(jnp.bfloat16)
    columns = modulated
    projected = jnp.einsum(
        "tsd,dhc->thsc",
        columns,
        lax.all_gather(qkv_weight, "seq", axis=0, tiled=True),
        preferred_element_type=jnp.float32,
    ).astype(jnp.bfloat16)
    pair_count = step_count * heads
    per_dev = pair_count // seq_devs
    grouped = projected.reshape(seq_devs, per_dev, tokd, width_three)
    routed = attend_pairs(lax.all_to_all(grouped, "seq", split_axis=0, concat_axis=2, tiled=True))
    returned = lax.all_to_all(routed, "seq", split_axis=2, concat_axis=0, tiled=True)
    flattened = jnp.transpose(
        returned.reshape(step_count, heads, tokd, hdim), (0, 2, 1, 3)
    ).reshape(step_count, tokd, width)
    columns = flattened
    projection = jnp.einsum(
        "tsd,de->tse",
        columns,
        lax.all_gather(out_weight, "seq", axis=0, tiled=True),
        preferred_element_type=jnp.float32,
    )
    updated = residual + gate_mod[:, None, :] * projection
    normed_out = layer_norm(updated).astype(jnp.bfloat16)
    noise_pred = jnp.einsum(
        "tsd,dc->tsc", normed_out, final_weight, preferred_element_type=jnp.float32
    )
    drift_terms = keep_coef[:, None, None] * previous + noise_coef[:, None, None] * noise_pred
    running_sums = jnp.cumsum(drift_terms, axis=0)
    block_total = running_sums[-1]
    carried = entering(block_total, "tm", add_terms, jnp.zeros_like(block_total))
    advanced = first_state[None] + carried[None] + running_sums
    difference = advanced - states
    partial_value = jnp.sum(difference * difference, axis=(1, 2))
    errors = lax.psum(partial_value, "seq") / (tokd * seq_devs * chans)
    return (advanced, errors)


def solution(mesh):
    in_specs = (
        P("tm", "seq", None),
        P("seq", None),
        P("tm"),
        P("tm"),
        P(),
        P(),
        P("seq", None, None),
        P("seq", None),
        P(),
    )
    out_specs = (P("tm", "seq", None), P("tm"))
    return jax.shard_map(
        per_device, mesh=mesh, in_specs=in_specs, out_specs=out_specs, check_vma=False
    )
```

profile of v0, /device:TPU:1, one launch (start us, length us, event | category | flops | bytes accessed | tf_op | source)
XLA Modules:
  0.0 330.8 jit_solution(13507943861712329472)
XLA Ops:
  8.8 4.3 %collective-permute-start = (f32[48,64]{1,0:T(8,128)S(1)}, f32[48,64]{1,0:T(8,128)S(1)}, u32[]{:S(2)}, u32[]{:S(2)}) collective-permute-start(f32[48,64]{1,0:T(8,128)S(1)} %slice_bitcast_fusion), channel_id=1, source_target_pairs={{0,32},{32,64},{64,96},{96,128},{128,160},{160,192},{192,224},{1,3... | collective-permute-start | bytes 36872 | tf_op jit(solution)/shard_map/ppermute | solution.py:11
  16.2 1.4 copy-done.1
  18.0 68.3 %all-gather.3.cloned.1.call-done = bf16[1536,12,384]{2,0,1:T(8,128)(2,1)} async-done(((bf16[48,12,384]{2,0,1:T(8,128)(2,1)}), bf16[1536,12,384]{2,0,1:T(8,128)(2,1)}) %all-gather.3.cloned.1.call-update) | async-done | bytes 14155792 | tf_op jit(solution)/shard_map/all_gather | solution.py:122
  86.3 11.1 %fusion.18 = bf16[8,48,12,384]{3,1,2,0:T(8,128)(2,1)} fusion(bf16[1536,12,384]{2,0,1:T(8,128)(2,1)} %all-gather.3.cloned.1.call-done, f32[8,48,1536]{2,1,0:T(8,128)} %copy-done.1, f32[8,1536]{1,0:T(8,128)S(1)} %get-tuple-element.105, f32[8,1536]{1,0:T(8,128)S(1)} %get-tuple-element.106, f32[8,48]{1,0:T(8,128)S(1)} %add_rsqrt_fusion.1, ...), kind=kOutput, calls=%fused_computation.20 | convolution fusion | flops 5440536576 | bytes 20155392 | tf_op jit(solution)/shard_map/tsd,dhc->thsc/dot_general | solution.py:119
  97.3 5.5 %all-to-all-start = ((bf16[32,3,48,384]{3,2,1,0:T(8,128)(2,1)}), bf16[32,3,48,384]{3,2,1,0:T(8,128)(2,1)}, u32[]{:S(2)}, u32[]{:S(2)}) async-start(bf16[32,3,48,384]{3,2,1,0:T(8,128)(2,1)} %bitcast.93), calls=%async_computation | async-start | bytes 7077888 | tf_op jit(solution)/shard_map/all_to_all | solution.py:128
  103.6 44.9 %all-to-all-done = bf16[32,3,48,384]{3,2,1,0:T(8,128)(2,1)} async-done(((bf16[32,3,48,384]{3,2,1,0:T(8,128)(2,1)}), bf16[32,3,48,384]{3,2,1,0:T(8,128)(2,1)}, u32[]{:S(2)}, u32[]{:S(2)}) %all-to-all-start) | async-done | bytes 3538976 | tf_op jit(solution)/shard_map/all_to_all | solution.py:128
  148.5 4.1 %copy.17 = bf16[1,3,32,48,384]{4,3,2,1,0:T(8,128)(2,1)} copy(bf16[1,3,32,48,384]{4,3,1,2,0:T(8,128)(2,1)} %bitcast.15) | data formatting | bytes 7077888 | tf_op jit(solution)/shard_map/all_to_all | solution.py:128
  152.6 33.7 %while.31 = (s32[]{:T(128)}, bf16[3,1536,128]{2,1,0:T(8,128)(2,1)}, bf16[3,1536,384]{2,1,0:T(8,128)(2,1)}, s32[]{:T(128)}, s32[]{:T(128)}, /*index=5*/s32[]{:T(128)}) while((s32[]{:T(128)}, bf16[3,1536,128]{2,1,0:T(8,128)(2,1)}, bf16[3,1536,384]{2,1,0:T(8,128)(2,1)}, s32[]{:T(128)}, s32[]{:T(128)}, /*index=5*/s32[]{:T(128)}) %tuple.79), condition=%wide.region_7.8_spmd, body=%wide.region_2.7_spmd.sunk | while | flops 408222720 | bytes 16002250 | solution.py:76
  152.6 1.4 dynamic-slice_bitcast_fusion.2
  154.2 7.8 %while.33 = (s32[]{:T(128)}, bf16[3,512,128]{2,1,0:T(8,128)(2,1)}, bf16[3,512,128]{2,1,0:T(8,128)(2,1)S(1)}, bf16[1536,128]{1,0:T(8,128)(2,1)S(1)}, bf16[1536,128]{1,0:T(8,128)(2,1)S(1)}, /*index=5*/s32[]{:T(128)}) while((s32[]{:T(128)}, bf16[3,512,128]{2,1,0:T(8,128)(2,1)}, bf16[3,512,128]{2,1,0:T(8,128)(2,1)S(1)}, ...), condition=%wide.region_6.6_spmd, body=%wide.region_3.5_spmd.sunk | while | flops 408222720 | bytes 10496585 | solution.py:71
  162.1 1.8 bitcast_dynamic-update-slice_fusion.2
  163.8 1.4 dynamic-slice_bitcast_fusion.2
  165.5 7.8 %while.33 = (s32[]{:T(128)}, bf16[3,512,128]{2,1,0:T(8,128)(2,1)}, bf16[3,512,128]{2,1,0:T(8,128)(2,1)S(1)}, bf16[1536,128]{1,0:T(8,128)(2,1)S(1)}, bf16[1536,128]{1,0:T(8,128)(2,1)S(1)}, /*index=5*/s32[]{:T(128)}) while((s32[]{:T(128)}, bf16[3,512,128]{2,1,0:T(8,128)(2,1)}, bf16[3,512,128]{2,1,0:T(8,128)(2,1)S(1)}, ...), condition=%wide.region_6.6_spmd, body=%wide.region_3.5_spmd.sunk | while | flops 408222720 | bytes 10496585 | solution.py:71
  173.3 1.8 bitcast_dynamic-update-slice_fusion.2
  176.7 7.8 %while.33 = (s32[]{:T(128)}, bf16[3,512,128]{2,1,0:T(8,128)(2,1)}, bf16[3,512,128]{2,1,0:T(8,128)(2,1)S(1)}, bf16[1536,128]{1,0:T(8,128)(2,1)S(1)}, bf16[1536,128]{1,0:T(8,128)(2,1)S(1)}, /*index=5*/s32[]{:T(128)}) while((s32[]{:T(128)}, bf16[3,512,128]{2,1,0:T(8,128)(2,1)}, bf16[3,512,128]{2,1,0:T(8,128)(2,1)S(1)}, ...), condition=%wide.region_6.6_spmd, body=%wide.region_3.5_spmd.sunk | while | flops 408222720 | bytes 10496585 | solution.py:71
  180.6 1.4 fusion.70
  184.6 1.8 bitcast_dynamic-update-slice_fusion.2
  186.3 8.1 %copy.31 = bf16[3,1536,128]{2,0,1:T(4,128)(2,1)} copy(bf16[3,1536,128]{2,1,0:T(8,128)(2,1)} %get-tuple-element.69) | data formatting | bytes 2359296 | tf_op jit(solution)/shard_map/while | solution.py:76
  194.4 7.4 %all-to-all-start.1 = ((bf16[1,3,1536,128]{3,1,0,2:T(4,128)(2,1)}), bf16[1,3,1536,128]{3,1,0,2:T(4,128)(2,1)}, u32[]{:S(2)}, u32[]{:S(2)}) async-start(bf16[1,3,1536,128]{3,1,0,2:T(4,128)(2,1)} %bitcast.91), calls=%async_computation.1 | async-start | bytes 3145728 | tf_op jit(solution)/shard_map/all_to_all | solution.py:129
  202.0 22.2 %all-to-all-done.1 = bf16[1,3,1536,128]{3,1,0,2:T(4,128)(2,1)} async-done(((bf16[1,3,1536,128]{3,1,0,2:T(4,128)(2,1)}), bf16[1,3,1536,128]{3,1,0,2:T(4,128)(2,1)}, u32[]{:S(2)}, u32[]{:S(2)}) %all-to-all-start.1) | async-done | bytes 1179680 | tf_op jit(solution)/shard_map/all_to_all | solution.py:129
  224.2 1.6 copy.19
  225.9 5.1 %fusion.55 = (f32[8,48]{1,0:T(8,128)S(1)}, f32[8,48,1536]{2,1,0:T(8,128)S(1)}) fusion(f32[8,48,1536]{2,1,0:T(8,128)} %copy-done.1, bf16[1536,1536]{1,0:T(8,128)(2,1)} %all-gather.5.cloned.1.call-done, bf16[8,12,6,8,128]{4,3,2,1,0:T(8,128)(2,1)S(1)} %bitcast.94, f32[8,1536]{1,0:T(8,128)} %get-tuple-element.104), kind=kOutput, calls=%fused_computation.77 | convolution fusion | flops 1813708416 | bytes 10667520 | tf_op jit(solution)/shard_map/tsd,de->tse/dot_general | solution.py:134
  232.6 20.1 %all_gather.11 = f32[8,48,64]{2,1,0:T(8,128)S(1)} all-gather(f32[1,48,64]{2,1,0:T(8,128)S(1)} %slice.39), channel_id=1, replica_groups=mesh['tm'=8,'seq'=32] {'tm'}, dimensions={0}, use_global_device_ids=true | all-gather | bytes 110592 | tf_op jit(solution)/shard_map/all_gather | solution.py:16
  253.5 70.0 %psum.7 = f32[8]{0:T(128)S(1)} all-reduce(f32[8]{0:T(128)S(1)} %get-tuple-element.95), channel_id=1, replica_groups=mesh['tm'=8,'seq'=32] {'seq'}, use_global_device_ids=true, to_apply=%region_14.15 | all-reduce | flops 8 | bytes 64 | tf_op jit(solution)/shard_map/psum | solution.py:152
  (93 shorter events, 32.7 us)
Async XLA Ops:
  7.2 6.7 %copy-start = (bf16[256,4608]{1,0:T(8,128)(2,1)S(1)}, bf16[256,4608]{1,0:T(8,128)(2,1)}, u32[]{:S(2)}) copy-start(bf16[256,4608]{1,0:T(8,128)(2,1)} %param.20) | copy-start | bytes 7077892
  7.2 7.8 %copy-start.4 = (f32[8,48,64]{2,1,0:T(8,128)S(1)}, f32[8,48,64]{2,1,0:T(8,128)}, u32[]{:S(2)}) copy-start(f32[8,48,64]{2,1,0:T(8,128)} %param.15) | copy-start | bytes 294916
  7.2 7.8 %copy-start.10 = (f32[48,64]{1,0:T(8,128)S(1)}, f32[48,64]{1,0:T(8,128)}, u32[]{:S(2)}) copy-start(f32[48,64]{1,0:T(8,128)} %param.16) | copy-start | bytes 36868
  7.2 8.4 %copy-start.9 = (bf16[64,1536]{1,0:T(8,128)(2,1)S(1)}, bf16[64,1536]{1,0:T(8,128)(2,1)}, u32[]{:S(2)}) copy-start(bf16[64,1536]{1,0:T(8,128)(2,1)} %param.19) | copy-start | bytes 589828
  7.2 79.0 %all-gather.3.cloned.1.call-start = ((), (), s32[]{:S(2)}) async-start(), calls=%async_computation.2 | async-start | bytes 14598144 | tf_op jit(solution)/shard_map/all_gather | solution.py:122
  8.8 6.2 %collective-permute-start = (f32[48,64]{1,0:T(8,128)S(1)}, f32[48,64]{1,0:T(8,128)S(1)}, u32[]{:S(2)}, u32[]{:S(2)}) collective-permute-start(f32[48,64]{1,0:T(8,128)S(1)} %slice_bitcast_fusion), channel_id=1, source_target_pairs={{0,32},{32,64},{64,96},{96,128},{128,160},{160,192},{192,224},{1,3... | collective-permute-start | bytes 36872 | tf_op jit(solution)/shard_map/ppermute | solution.py:11
  15.0 3.0 copy-start.2
  15.0 0.6 copy-start.6
  16.2 1.4 copy-start.1
  97.3 51.2 %all-to-all-start = ((bf16[32,3,48,384]{3,2,1,0:T(8,128)(2,1)}), bf16[32,3,48,384]{3,2,1,0:T(8,128)(2,1)}, u32[]{:S(2)}, u32[]{:S(2)}) async-start(bf16[32,3,48,384]{3,2,1,0:T(8,128)(2,1)} %bitcast.93), calls=%async_computation | async-start | bytes 7077888 | tf_op jit(solution)/shard_map/all_to_all | solution.py:128
  102.8 123.1 %all-gather.5.cloned.1.call-start = ((), (), s32[]{:S(2)}) async-start(), calls=%async_computation.3 | async-start | bytes 4866048 | tf_op jit(solution)/shard_map/all_gather | solution.py:137
  186.3 15.5 %copy-start.12 = (s32[8]{0:T(128)S(1)}, s32[8]{0:T(128)}, u32[]{:S(2)}) copy-start(s32[8]{0:T(128)} %param.17) | copy-start | bytes 100
  186.3 15.5 %copy-start.13 = (s32[8]{0:T(128)S(1)}, s32[8]{0:T(128)}, u32[]{:S(2)}) copy-start(s32[8]{0:T(128)} %param.18) | copy-start | bytes 100
  194.4 29.8 %all-to-all-start.1 = ((bf16[1,3,1536,128]{3,1,0,2:T(4,128)(2,1)}), bf16[1,3,1536,128]{3,1,0,2:T(4,128)(2,1)}, u32[]{:S(2)}, u32[]{:S(2)}) async-start(bf16[1,3,1536,128]{3,1,0,2:T(4,128)(2,1)} %bitcast.91), calls=%async_computation.1 | async-start | bytes 3145728 | tf_op jit(solution)/shard_map/all_to_all | solution.py:129
  231.0 0.9 copy-start.8
  231.1 1.5 copy-start.3
  231.1 1.4 copy-start.7
  231.5 21.3 %copy-start.11 = (f32[48,64]{1,0:T(8,128)S(1)}, f32[48,64]{1,0:T(8,128)}, u32[]{:S(2)}) copy-start(f32[48,64]{1,0:T(8,128)} %param.16) | copy-start | bytes 36868
  231.5 21.3 %copy-start.5 = (f32[8,48,64]{2,1,0:T(8,128)S(1)}, f32[8,48,64]{2,1,0:T(8,128)}, u32[]{:S(2)}) copy-start(f32[8,48,64]{2,1,0:T(8,128)} %param.15) | copy-start | bytes 294916
Sparse Core Ops, SparseCore 0:
  10.7 75.5 all-gather.2
  106.2 68.7 all-gather.4
where the time goes:
time: 331 us
  waiting for transfers between devices  137 us (41%)
  blocking collectives  90.1 us (27%)
  matrix products  36 us (11%)
  local copies, waits for them, and re-layouts  27.4 us (8%)
  starting transfers between devices  17.3 us (5%)
  between operations  14.4 us (4%)
  other arithmetic  8.79 us (3%)
    psum x1, blocking collectives, per_device(): errors = lax.psum(partial_value, 'seq') / (tokd * seq_devs * chans)  70 us
    all_gather x1, waiting for transfers between devices, per_device(): lax.all_gather(qkv_weight, 'seq', axis=0, tiled=True)  68.3 us
    all_to_all x1, waiting for transfers between devices, per_device(): lax.all_to_all(grouped, 'seq', split_axis=0, concat_axis=2, tiled=True)  44.9 us
    all_to_all x1, waiting for transfers between devices, per_device(): lax.all_to_all(routed, 'seq', split_axis=2, concat_axis=0, tiled=True)  22.2 us
    all_gather x1, blocking collectives, entering(): gathered = lax.all_gather(part, axis)  20.1 us
    dot_general x9, matrix products, one_block(): jnp.dot(weights, values, preferred_element_type=jnp.float32)  12.4 us
    dot_general x1, matrix products, per_device(): jnp.einsum('tsd,dhc->thsc', columns, lax.all_gather(qkv_weight, 'seq', ax...  11.1 us
    while x1, local copies, waits for them, and re-layouts, attend_pairs(): return lax.map(attend_one, pair_block[0])[None]  8.06 us
  transfers between devices with their start and end apart: 5, of which 3 were waited for; matrix products, arithmetic and copies ran while one was open for 15% of the time, Pallas kernels for 0%

commit v1 on v0

--- a/solution.py
+++ b/solution.py
@@ -1,8 +1,18 @@
+import functools
 import math
 import jax
 import jax.numpy as jnp
 from jax import lax
 from jax.sharding import PartitionSpec as P
+
+
+def _place_stacks_all(row_data, row_axis, at_axis):
+    response = lax.axis_size(row_axis)
+    kept_arr = lax.all_to_all(jnp.stack(response * [row_data]), row_axis, 0, 0)
+    return jnp.concatenate(kept_arr, at_axis)
+
+
+search_core = functools.partial(_place_stacks_all, row_axis="seq", at_axis=0)
 
 
 def from_behind(shard, axis, by):
@@ -117,10 +127,7 @@
     ).astype(jnp.bfloat16)
     columns = modulated
     projected = jnp.einsum(
-        "tsd,dhc->thsc",
-        columns,
-        lax.all_gather(qkv_weight, "seq", axis=0, tiled=True),
-        preferred_element_type=jnp.float32,
+        "tsd,dhc->thsc", columns, search_core(qkv_weight), preferred_element_type=jnp.float32
     ).astype(jnp.bfloat16)
     pair_count = step_count * heads
     per_dev = pair_count // seq_devs

time: 331 us -> 444 us (1.34)
  waiting for transfers between devices: 137 us -> 232 us
  starting transfers between devices: 17.3 us -> 33.9 us
  matrix products: 36 us -> 26.3 us
  local copies, waits for them, and re-layouts: 27.4 us -> 35.3 us
    all_to_all x0 -> x1, waiting for transfers between devices: none -> 164 us  [_place_stacks_all(): kept_arr = lax.all_to_all(jnp.stack(response * [row_data]), row_axis, 0, 0)]
    all_gather x1 -> x0, waiting for transfers between devices: 68.3 us -> none  [per_device(): lax.all_gather(qkv_weight, 'seq', axis=0, tiled=True)]
    all_to_all x1, starting transfers between devices: 5.48 us -> 14.2 us  [per_device(): lax.all_to_all(grouped, 'seq', split_axis=0, concat_axis=2, tiled=True)]
    all_to_all x0 -> x1, starting transfers between devices: none -> 8.76 us  [_place_stacks_all(): kept_arr = lax.all_to_all(jnp.stack(response * [row_data]), row_axis, 0, 0)]
    another operation x0 -> x1, local copies, waits for them, and re-layouts: none -> 8.4 us  [_place_stacks_all(): kept_arr = lax.all_to_all(jnp.stack(response * [row_data]), row_axis, 0, 0)]
    all_to_all x0 -> x1, local copies, waits for them, and re-layouts: none -> 6.77 us  [_place_stacks_all(): kept_arr = lax.all_to_all(jnp.stack(response * [row_data]), row_axis, 0, 0)]
    dot_general x9, matrix products: 12.4 us -> 6.97 us  [one_block(): jnp.dot(weights, values, preferred_element_type=jnp.float32)]
    dynamic_update_slice x3, local copies, waits for them, and re-layouts: 5.33 us -> 0.17 us  [attend_pairs(): return lax.map(attend_one, pair_block[0])[None]]
  transfers between devices with their start and end apart: 5 -> 5, of which waited for: 3 -> 3; matrix products, arithmetic and copies ran while one was open for 15% -> 9% of each run, Pallas kernels for 0% -> 0%
where the time goes in v1:
time: 444 us; the launch traced here: 443 us
  waiting for transfers between devices  232 us (52%)
  blocking collectives  93 us (21%)
  local copies, waits for them, and re-layouts  35.3 us (8%)
  starting transfers between devices  33.9 us (8%)
  matrix products  26.3 us (6%)
  between operations  14.5 us (3%)
  other arithmetic  8.14 us (2%)
    all_to_all x1, waiting for transfers between devices, _place_stacks_all(): kept_arr = lax.all_to_all(jnp.stack(response * [row_data]), row_axis, 0, 0)  164 us
    psum x1, blocking collectives, per_device(): errors = lax.psum(partial_value, 'seq') / (tokd * seq_devs * chans)  70.3 us
    all_to_all x1, waiting for transfers between devices, per_device(): lax.all_to_all(grouped, 'seq', split_axis=0, concat_axis=2, tiled=True)  44.9 us
    all_gather x1, blocking collectives, entering(): gathered = lax.all_gather(part, axis)  22.7 us
    all_to_all x1, waiting for transfers between devices, per_device(): lax.all_to_all(routed, 'seq', split_axis=2, concat_axis=0, tiled=True)  22.2 us
    all_to_all x1, starting transfers between devices, per_device(): lax.all_to_all(grouped, 'seq', split_axis=0, concat_axis=2, tiled=True)  14.2 us
  transfers between devices with their start and end apart: 5, of which 3 were waited for; matrix products, arithmetic and copies ran while one was open for 9% of the time, Pallas kernels for 0%

profile of v1, /device:TPU:1, one launch (start us, length us, event | category | flops | bytes accessed | tf_op | source)
XLA Modules:
  0.0 443.2 jit_solution(602182317919827615)
XLA Ops:
  7.2 8.4 %stack.2 = bf16[32,48,12,384]{3,1,2,0:T(8,128)(2,1)} broadcast(bf16[48,12,384]{2,0,1:T(8,128)(2,1)} %param.21), dimensions={1,2,3} | broadcast | bytes 14598144 | tf_op jit(solution)/shard_map/stack | solution.py:11
  15.6 8.8 %all-to-all-start = ((bf16[32,48,12,384]{3,1,2,0:T(8,128)(2,1)}), bf16[32,48,12,384]{3,1,2,0:T(8,128)(2,1)}, u32[]{:S(2)}, u32[]{:S(2)}) async-start(bf16[32,48,12,384]{3,1,2,0:T(8,128)(2,1)} %stack.2), calls=%async_computation | async-start | bytes 28311552 | tf_op jit(solution)/shard_map/all_to_all | solution.py:11
  24.4 3.7 collective-permute-start
  30.9 164.2 %all-to-all-done = bf16[32,48,12,384]{3,1,2,0:T(8,128)(2,1)} async-done(((bf16[32,48,12,384]{3,1,2,0:T(8,128)(2,1)}), bf16[32,48,12,384]{3,1,2,0:T(8,128)(2,1)}, u32[]{:S(2)}, u32[]{:S(2)}) %all-to-all-start) | async-done | bytes 14155808 | tf_op jit(solution)/shard_map/all_to_all | solution.py:11
  195.1 6.8 %copy.17 = bf16[32,48,12,384]{3,1,0,2:T(8,128)(2,1)S(1)} copy(bf16[32,48,12,384]{3,1,2,0:T(8,128)(2,1)} %all-to-all-done) | data formatting | bytes 28311552 | tf_op jit(solution)/shard_map/all_to_all | solution.py:11
  201.9 7.6 %convolution_convert_fusion = bf16[8,48,12,384]{3,1,2,0:T(8,128)(2,1)} fusion(bf16[1536,12,384,1]{2,0,1,3:T(8,128)(2,1)S(1)} %bitcast.90, f32[8,48,1536]{2,1,0:T(8,128)S(1)} %get-tuple-element.110, f32[8,1536]{1,0:T(8,128)S(1)} %get-tuple-element.105, f32[8,1536]{1,0:T(8,128)S(1)} %get-tuple-element.106, f32[8,48]{1,0:T(8,128)S(1)} %add_rsqrt_fusion.1, ...), kind=kOutput, calls=%fused_computation.18 | convolution fusion | flops 5440536576 | bytes 20155392 | tf_op jit(solution)/shard_map/tsd,dhc->thsc/dot_general | solution.py:129
  209.4 14.2 %all-to-all-start.1 = ((bf16[32,3,48,384]{3,2,1,0:T(8,128)(2,1)}), bf16[32,3,48,384]{3,2,1,0:T(8,128)(2,1)}, u32[]{:S(2)}, u32[]{:S(2)}) async-start(bf16[32,3,48,384]{3,2,1,0:T(8,128)(2,1)} %bitcast.93), calls=%async_computation.1 | async-start | bytes 7077888 | tf_op jit(solution)/shard_map/all_to_all | solution.py:135
  224.4 44.9 %all-to-all-done.1 = bf16[32,3,48,384]{3,2,1,0:T(8,128)(2,1)} async-done(((bf16[32,3,48,384]{3,2,1,0:T(8,128)(2,1)}), bf16[32,3,48,384]{3,2,1,0:T(8,128)(2,1)}, u32[]{:S(2)}, u32[]{:S(2)}) %all-to-all-start.1) | async-done | bytes 3538976 | tf_op jit(solution)/shard_map/all_to_all | solution.py:135
  269.3 4.1 copy.18
  273.4 23.3 %while.31 = (s32[]{:T(128)}, bf16[3,1536,128]{2,1,0:T(8,128)(2,1)S(1)}, bf16[3,1536,384]{2,1,0:T(8,128)(2,1)}, s32[]{:T(128)}, s32[]{:T(128)}, /*index=5*/s32[]{:T(128)}) while((s32[]{:T(128)}, bf16[3,1536,128]{2,1,0:T(8,128)(2,1)S(1)}, bf16[3,1536,384]{2,1,0:T(8,128)(2,1)}, s32[]{:T(128)}, s32[]{:T(128)}, /*index=5*/s32[]{:T(128)}) %tuple.77), condition=%wide.region_7.8_spmd, body=%wide.region_2.7_spmd.sunk | while | flops 408222720 | bytes 16001234 | solution.py:86
  273.4 1.4 dynamic-slice_bitcast_fusion.2
  275.0 6.1 %while.33 = (s32[]{:T(128)}, bf16[3,512,128]{2,1,0:T(8,128)(2,1)S(1)}, bf16[3,512,128]{2,1,0:T(8,128)(2,1)S(1)}, bf16[1536,128]{1,0:T(8,128)(2,1)S(1)}, bf16[1536,128]{1,0:T(8,128)(2,1)S(1)}, /*index=5*/s32[]{:T(128)}) while((s32[]{:T(128)}, bf16[3,512,128]{2,1,0:T(8,128)(2,1)S(1)}, bf16[3,512,128]{2,1,0:T(8,128)(2,1)S(1)}, ...), condition=%wide.region_6.6_spmd, body=%wide.region_3.5_spmd.sunk | while | flops 408222720 | bytes 10496077 | solution.py:81
  276.3 0.8 fusion.66
  281.2 1.4 dynamic-slice_bitcast_fusion.2
  282.8 6.1 %while.33 = (s32[]{:T(128)}, bf16[3,512,128]{2,1,0:T(8,128)(2,1)S(1)}, bf16[3,512,128]{2,1,0:T(8,128)(2,1)S(1)}, bf16[1536,128]{1,0:T(8,128)(2,1)S(1)}, bf16[1536,128]{1,0:T(8,128)(2,1)S(1)}, /*index=5*/s32[]{:T(128)}) while((s32[]{:T(128)}, bf16[3,512,128]{2,1,0:T(8,128)(2,1)S(1)}, bf16[3,512,128]{2,1,0:T(8,128)(2,1)S(1)}, ...), condition=%wide.region_6.6_spmd, body=%wide.region_3.5_spmd.sunk | while | flops 408222720 | bytes 10496077 | solution.py:81
  289.0 1.4 dynamic-slice_bitcast_fusion.2
  290.6 6.1 %while.33 = (s32[]{:T(128)}, bf16[3,512,128]{2,1,0:T(8,128)(2,1)S(1)}, bf16[3,512,128]{2,1,0:T(8,128)(2,1)S(1)}, bf16[1536,128]{1,0:T(8,128)(2,1)S(1)}, bf16[1536,128]{1,0:T(8,128)(2,1)S(1)}, /*index=5*/s32[]{:T(128)}) while((s32[]{:T(128)}, bf16[3,512,128]{2,1,0:T(8,128)(2,1)S(1)}, bf16[3,512,128]{2,1,0:T(8,128)(2,1)S(1)}, ...), condition=%wide.region_6.6_spmd, body=%wide.region_3.5_spmd.sunk | while | flops 408222720 | bytes 10496077 | solution.py:81
  296.7 8.2 %copy.32 = bf16[3,1536,128]{2,0,1:T(4,128)(2,1)} copy(bf16[3,1536,128]{2,1,0:T(8,128)(2,1)S(1)} %get-tuple-element.69) | data formatting | bytes 2359296 | tf_op jit(solution)/shard_map/while | solution.py:86
  304.9 7.0 %all-to-all-start.2 = ((bf16[1,3,1536,128]{3,1,0,2:T(4,128)(2,1)}), bf16[1,3,1536,128]{3,1,0,2:T(4,128)(2,1)}, u32[]{:S(2)}, u32[]{:S(2)}) async-start(bf16[1,3,1536,128]{3,1,0,2:T(4,128)(2,1)} %bitcast.71), calls=%async_computation.2 | async-start | bytes 3145728 | tf_op jit(solution)/shard_map/all_to_all | solution.py:136
  312.1 22.2 %all-to-all-done.2 = bf16[1,3,1536,128]{3,1,0,2:T(4,128)(2,1)} async-done(((bf16[1,3,1536,128]{3,1,0,2:T(4,128)(2,1)}), bf16[1,3,1536,128]{3,1,0,2:T(4,128)(2,1)}, u32[]{:S(2)}, u32[]{:S(2)}) %all-to-all-start.2) | async-done | bytes 1179680 | tf_op jit(solution)/shard_map/all_to_all | solution.py:136
  334.3 1.6 copy.20
  336.0 4.4 fusion.50
  342.0 22.7 %all_gather.7 = f32[8,48,64]{2,1,0:T(8,128)S(1)} all-gather(f32[1,48,64]{2,1,0:T(8,128)S(1)} %slice.39), channel_id=1, replica_groups=mesh['tm'=8,'seq'=32] {'tm'}, dimensions={0}, use_global_device_ids=true | all-gather | bytes 110592 | tf_op jit(solution)/shard_map/all_gather | solution.py:26
  365.5 70.3 %psum.7 = f32[8]{0:T(128)S(1)} all-reduce(f32[8]{0:T(128)S(1)} %get-tuple-element.95), channel_id=1, replica_groups=mesh['tm'=8,'seq'=32] {'seq'}, use_global_device_ids=true, to_apply=%region_14.15 | all-reduce | flops 8 | bytes 64 | tf_op jit(solution)/shard_map/psum | solution.py:159
  (100 shorter events, 24.5 us)
Async XLA Ops:
  7.2 21.1 %copy-start = (bf16[256,4608]{1,0:T(8,128)(2,1)S(1)}, bf16[256,4608]{1,0:T(8,128)(2,1)}, u32[]{:S(2)}) copy-start(bf16[256,4608]{1,0:T(8,128)(2,1)} %param.20) | copy-start | bytes 7077892
  15.6 8.8 %copy-start.6 = (f32[8,48,64]{2,1,0:T(8,128)S(1)}, f32[8,48,64]{2,1,0:T(8,128)}, u32[]{:S(2)}) copy-start(f32[8,48,64]{2,1,0:T(8,128)} %param.15) | copy-start | bytes 294916
  15.6 12.5 %copy-start.14 = (s32[8]{0:T(128)S(1)}, s32[8]{0:T(128)}, u32[]{:S(2)}) copy-start(s32[8]{0:T(128)} %param.17) | copy-start | bytes 100
  15.6 179.5 %all-to-all-start = ((bf16[32,48,12,384]{3,1,2,0:T(8,128)(2,1)}), bf16[32,48,12,384]{3,1,2,0:T(8,128)(2,1)}, u32[]{:S(2)}, u32[]{:S(2)}) async-start(bf16[32,48,12,384]{3,1,2,0:T(8,128)(2,1)} %stack.2), calls=%async_computation | async-start | bytes 28311552 | tf_op jit(solution)/shard_map/all_to_all | solution.py:11
  24.4 5.0 %copy-start.12 = (f32[48,64]{1,0:T(8,128)S(1)}, f32[48,64]{1,0:T(8,128)}, u32[]{:S(2)}) copy-start(f32[48,64]{1,0:T(8,128)} %param.16) | copy-start | bytes 36868
  24.4 5.6 %copy-start.11 = (bf16[64,1536]{1,0:T(8,128)(2,1)S(1)}, bf16[64,1536]{1,0:T(8,128)(2,1)}, u32[]{:S(2)}) copy-start(bf16[64,1536]{1,0:T(8,128)(2,1)} %param.19) | copy-start | bytes 589828
  24.4 4.9 %collective-permute-start = (f32[48,64]{1,0:T(8,128)S(1)}, f32[48,64]{1,0:T(8,128)S(1)}, u32[]{:S(2)}, u32[]{:S(2)}) collective-permute-start(f32[48,64]{1,0:T(8,128)S(1)} %slice_bitcast_fusion), channel_id=1, source_target_pairs={{0,32},{32,64},{64,96},{96,128},{128,160},{160,192},{192,224},{1,3... | collective-permute-start | bytes 36872 | tf_op jit(solution)/shard_map/ppermute | solution.py:21
  29.3 1.6 copy-start.4
  29.4 0.6 copy-start.8
  30.5 171.4 %copy-start.2 = (f32[8,48,1536]{2,1,0:T(8,128)}, f32[8,48,1536]{2,1,0:T(8,128)S(1)}, u32[]{:S(2)}) copy-start(f32[8,48,1536]{2,1,0:T(8,128)S(1)} %get-tuple-element.110) | copy-start | bytes 7077892
  209.4 59.9 %all-to-all-start.1 = ((bf16[32,3,48,384]{3,2,1,0:T(8,128)(2,1)}), bf16[32,3,48,384]{3,2,1,0:T(8,128)(2,1)}, u32[]{:S(2)}, u32[]{:S(2)}) async-start(bf16[32,3,48,384]{3,2,1,0:T(8,128)(2,1)} %bitcast.93), calls=%async_computation.1 | async-start | bytes 7077888 | tf_op jit(solution)/shard_map/all_to_all | solution.py:135
  223.7 112.3 %all-gather.2.cloned.1.call-start = ((), (), s32[]{:S(2)}) async-start(), calls=%async_computation.3 | async-start | bytes 4866048 | tf_op jit(solution)/shard_map/all_gather | solution.py:144
  296.7 15.2 %copy-start.15 = (s32[8]{0:T(128)S(1)}, s32[8]{0:T(128)}, u32[]{:S(2)}) copy-start(s32[8]{0:T(128)} %param.17) | copy-start | bytes 100
  296.7 15.2 %copy-start.16 = (s32[8]{0:T(128)S(1)}, s32[8]{0:T(128)}, u32[]{:S(2)}) copy-start(s32[8]{0:T(128)} %param.18) | copy-start | bytes 100
  304.9 29.4 %all-to-all-start.2 = ((bf16[1,3,1536,128]{3,1,0,2:T(4,128)(2,1)}), bf16[1,3,1536,128]{3,1,0,2:T(4,128)(2,1)}, u32[]{:S(2)}, u32[]{:S(2)}) async-start(bf16[1,3,1536,128]{3,1,0,2:T(4,128)(2,1)} %bitcast.71), calls=%async_computation.2 | async-start | bytes 3145728 | tf_op jit(solution)/shard_map/all_to_all | solution.py:136
  312.1 23.9 %copy-start.3 = (f32[8,48,1536]{2,1,0:T(8,128)S(1)}, f32[8,48,1536]{2,1,0:T(8,128)}, u32[]{:S(2)}) copy-start(f32[8,48,1536]{2,1,0:T(8,128)} %copy-done.2) | copy-start | bytes 7077892
  340.4 0.9 copy-start.10
  340.5 1.4 copy-start.5
  340.5 1.4 copy-start.9
  340.9 23.9 %copy-start.13 = (f32[48,64]{1,0:T(8,128)S(1)}, f32[48,64]{1,0:T(8,128)}, u32[]{:S(2)}) copy-start(f32[48,64]{1,0:T(8,128)} %param.16) | copy-start | bytes 36868
  340.9 23.9 %copy-start.7 = (f32[8,48,64]{2,1,0:T(8,128)S(1)}, f32[8,48,64]{2,1,0:T(8,128)}, u32[]{:S(2)}) copy-start(f32[8,48,64]{2,1,0:T(8,128)} %param.15) | copy-start | bytes 294916
  340.9 95.5 %copy-start.1 = (bf16[256,4608]{1,0:T(8,128)(2,1)S(1)}, bf16[256,4608]{1,0:T(8,128)(2,1)}, u32[]{:S(2)}) copy-start(bf16[256,4608]{1,0:T(8,128)(2,1)} %param.20) | copy-start | bytes 7077892
Sparse Core Ops, SparseCore 0:
  227.0 70.1 all-gather.1
